TPU v7x, 32 devices: a whole 2x2x4 slice. The times are simulated.
32 devices in a mesh: shot: 2 (over y), gy: 4 (over z), gx: 4 (over x, core).
Axes of the slice: x: 2, y: 2, z: 4, core: 2. Of those that a mesh axis runs over, the one named last changes fastest.
Arguments:
- pressure_now: float32 [128, 64, 512], P(('shot', 'gx'), 'gy'), parts along dimension 0, may hold values from -6 to 6
- pressure_old: float32 [128, 64, 512], P(('shot', 'gx'), 'gy'), parts along dimension 0, may hold values from -6 to 6
- classes: int32 [128, 64, 512], P(('shot', 'gx'), 'gy'), parts along dimension 0, may hold values from 0 to 15
- class_table: float32 [16], replicated, may hold values from 0.02 to 0.19
- wavelet: float32 [512], P('shot'), parts along dimension 0, may hold values from -12 to 12
- source_cells: int32 [8], P('shot'), parts along dimension 0, may hold values from 0 to 2097151
- samples: int32 [8], P('shot'), parts along dimension 0, may hold values from 0 to 255
Outputs:
- pressure_next: float32 [128, 64, 512], P(('shot', 'gx'), 'gy'), parts along dimension 0
- pressure_mid: float32 [128, 64, 512], P(('shot', 'gx'), 'gy'), parts along dimension 0
- snapshot_code: float32 [128, 64, 512], P(('shot', 'gx'), 'gy'), parts along dimension 0
There are 2 independent parts, one for each index of `shot`. A program takes and returns all parts, laid end to end along the dimension named above; an argument that names none is the same for every part. Nothing has to cross between parts.
Inputs may be any that keep to these rules, and one draw needn't show every extreme that they name: `source_cells`: decoded as ix * 64 * 512 + iy * 512 + iz.
All inputs are finite; a program needn't handle non-finite values.
Results may differ from a plain program's by a relative error of at most 0.0003.
Values sent between devices are 32-bit elements; how exact they have to be, the bound alone decides.
No kernel may reach another device: no remote copies, remote signals or barrier semaphores. Data moves between devices by JAX's collectives and lax.ppermute only.
A program may use at most 64 MiB of HBM per device.

v0:
```python
import functools

import jax
import jax.numpy as jnp
from jax import lax
from jax.experimental import pallas as pl
from jax.experimental.pallas import tpu as pltpu
from jax.sharding import PartitionSpec as P


STENCIL_WEIGHTS = (-205.0 / 72.0, 8.0 / 5.0, -1.0 / 5.0, 8.0 / 315.0, -1.0 / 560.0)
LIFT_ALPHA = -1.586134342
LIFT_BETA = -0.05298011854
LIFT_GAMMA = 0.8829110762
LIFT_DELTA = 0.4435068522
LIFT_SCALE = 1.149604398
DEAD_ZONE = 0.25
QUANT_STEP = 0.5

HALO = 4
LANES = 128
SUB = 8


def iota(axis):
    return lax.broadcasted_iota(jnp.int32, (SUB, LANES), axis)


def rolled(value, shift, axis):
    size = value.shape[axis]
    shift = shift % size
    return value if shift == 0 else pltpu.roll(value, shift, axis)


def parity(axis):
    index = lax.axis_index(axis)
    return lax.rem(index, 2) == 0, index == 0, index == lax.axis_size(axis) - 1


def pack_x(field, low, high, even, x_first, x_second):
    for slot, (down, up) in enumerate(zip(low, high)):
        for tile in range(x_first.shape[1]):
            for y_tile in range(x_first.shape[2] // SUB):
                below, above = field(down, tile, y_tile), field(up, tile, y_tile)
                where = (slot, tile, pl.ds(y_tile * SUB, SUB))
                x_first[where] = jnp.where(even, above, below)
                x_second[where] = jnp.where(even, below, above)


def pack_y(rows, rows_x, tiles, even, y_first, y_second):
    def step(x, _):
        for tile in range(tiles):
            below, above = rows(x, tile)
            where = (x, tile // 2, pl.ds(tile % 2 * HALO, HALO))
            y_first[where] = jnp.where(even, above, below)
            y_second[where] = jnp.where(even, below, above)
        return 0

    lax.fori_loop(0, rows_x, step, 0, unroll=4)


def zero_pads(padded, rows_x, rows_y):
    zero = jnp.zeros((SUB, LANES), jnp.float32)
    tiles = padded.shape[1]
    for x in list(range(HALO)) + list(range(rows_x + HALO, rows_x + 2 * HALO)):
        for tile in range(tiles):
            for y in range(SUB, rows_y + SUB, SUB):
                padded[x, tile, pl.ds(y, SUB)] = zero

    def step(x, _):
        for tile in range(tiles):
            padded[x + HALO, tile, pl.ds(0, SUB)] = zero
            padded[x + HALO, tile, pl.ds(rows_y + SUB, SUB)] = zero
        return 0

    lax.fori_loop(0, rows_x, step, 0)


def padded_vector(padded):
    return lambda x, tile, y_tile: padded[x + HALO, tile, pl.ds(SUB + y_tile * SUB, SUB)]


def sends_kernel(now, x_first, x_second, y_first, y_second):
    rows_x, rows_y, depth = now.shape
    even_x, _, _ = parity("gx")
    even_y, _, _ = parity("gy")

    def field(x, tile, y_tile):
        return now[x, pl.ds(y_tile * SUB, SUB), pl.ds(tile * LANES, LANES)]

    pack_x(field, range(HALO), range(rows_x - HALO, rows_x), even_x, x_first, x_second)

    def rows(x, tile):
        z = pl.ds(tile * LANES, LANES)
        return now[x, pl.ds(0, HALO), z], now[x, pl.ds(rows_y - HALO, HALO), z]

    pack_y(rows, rows_x, depth // LANES, even_y, y_first, y_second)


def local_laplace(padded, x, tiles, y_tile):
    lane = iota(1)
    row, y = x + HALO, SUB + y_tile * SUB
    center = [padded[row, tile, pl.ds(y, SUB)] for tile in range(tiles)]
    zero = jnp.zeros((SUB, LANES), jnp.float32)
    total = [3.0 * STENCIL_WEIGHTS[0] * value for value in center]
    for offset in range(1, HALO + 1):
        up = [rolled(value, -offset, 1) for value in center] + [zero]
        down = [zero] + [rolled(value, offset, 1) for value in center]
        for tile in range(tiles):
            beside = jnp.where(lane < LANES - offset, up[tile], up[tile + 1])
            beside = beside + jnp.where(lane >= offset, down[tile + 1], down[tile])
            beside = beside + (
                padded[row + offset, tile, pl.ds(y, SUB)]
                + padded[row - offset, tile, pl.ds(y, SUB)]
            )
            beside = beside + (
                padded[row, tile, pl.ds(y + offset, SUB)]
                + padded[row, tile, pl.ds(y - offset, SUB)]
            )
            total[tile] = total[tile] + STENCIL_WEIGHTS[offset] * beside
    return center, total


def add_sources(base, cells, samples, wavelet, step_index, rows_x, rows_y, depth):
    all_y = rows_y * lax.axis_size("gy")
    start_x = lax.axis_index("gx") * rows_x
    start_y = lax.axis_index("gy") * rows_y
    lane = lax.broadcasted_iota(jnp.int32, (1, LANES), 1)
    for shot in range(cells.shape[0]):
        cell = cells[shot]
        x = lax.div(cell, all_y * depth) - start_x
        y = lax.rem(lax.div(cell, depth), all_y) - start_y
        z = lax.rem(cell, depth)
        inside = (x >= 0) & (x < rows_x) & (y >= 0) & (y < rows_y)

        @pl.when(inside)
        def _():
            value = wavelet[lax.rem(samples[shot] + step_index, wavelet.shape[0])]
            where = (x, lax.div(z, LANES), pl.ds(y, 1))
            base[where] = base[where] + jnp.where(lane == lax.rem(z, LANES), value, 0.0)


def start_all(copies):
    for copy in copies:
        copy.start()
    return copies


def wait_all(copies):
    for copy in copies:
        copy.wait()


def paired(sources, targets, sems):
    return [
        pltpu.make_async_copy(source, target, sems.at[place])
        for place, (source, target) in enumerate(zip(sources, targets))
    ]


def first_local_kernel(
    now, old, classes, table, wavelet, cells, samples,
    padded, base, courant, blank,
    old_here, classes_here, table_here, wavelet_here, cells_here, samples_here, sems,
):
    rows_x, rows_y, depth = old.shape
    tiles = depth // LANES
    lane = iota(1)
    copies = start_all(
        paired(
            (table, classes, old, wavelet, cells, samples),
            (table_here, classes_here, old_here, wavelet_here, cells_here, samples_here),
            sems,
        )
    )
    zero_pads(padded, rows_x, rows_y)

    def spread(x, _):
        for tile in range(tiles):
            for y in range(0, rows_y, SUB):
                padded[x + HALO, tile, pl.ds(SUB + y, SUB)] = now[
                    x, pl.ds(y, SUB), pl.ds(tile * LANES, LANES)
                ]
        return 0

    lax.fori_loop(0, rows_x, spread, 0, unroll=4)

    def sums(x, _):
        for y_tile in range(rows_y // SUB):
            _, total = local_laplace(padded, x, tiles, y_tile)
            for tile in range(tiles):
                base[x, tile, pl.ds(y_tile * SUB, SUB)] = total[tile]
        return 0

    lax.fori_loop(0, rows_x, sums, 0, unroll=4)
    wait_all(copies)
    entries = jnp.zeros((SUB, LANES), jnp.float32)
    for material in range(table.shape[0]):
        entries = jnp.where(lane == material, table_here[material], entries)

    def step(x, _):
        for y_tile in range(rows_y // SUB):
            y = pl.ds(y_tile * SUB, SUB)
            for tile in range(tiles):
                z = pl.ds(tile * LANES, LANES)
                speed = jnp.take_along_axis(entries, classes_here[x, y, z], axis=1)
                courant[x, tile, y] = speed
                base[x, tile, y] = (
                    2.0 * now[x, y, z] - old_here[x, y, z] + speed * base[x, tile, y]
                )
        return 0

    lax.fori_loop(0, rows_x, step, 0, unroll=4)
    add_sources(
        base, cells_here, samples_here, wavelet_here, 0, rows_x, rows_y, depth
    )
    zero_pads(blank, rows_x, rows_y)


def second_local_kernel(
    padded, before, courant, wavelet, cells, samples,
    base, mid,
    wavelet_here, cells_here, samples_here, sems,
):
    rows_x, rows_y, depth = mid.shape
    tiles = depth // LANES
    copies = start_all(
        paired(
            [wavelet, cells, samples]
            + [padded.at[pl.ds(HALO, rows_x), t, pl.ds(SUB, rows_y), :] for t in range(tiles)],
            [wavelet_here, cells_here, samples_here]
            + [mid.at[:, :, pl.ds(t * LANES, LANES)] for t in range(tiles)],
            sems,
        )
    )

    def step(x, _):
        for y_tile in range(rows_y // SUB):
            center, total = local_laplace(padded, x, tiles, y_tile)
            y = pl.ds(y_tile * SUB, SUB)
            for tile in range(tiles):
                earlier = before[x + HALO, tile, pl.ds(SUB + y_tile * SUB, SUB)]
                base[x, tile, y] = (
                    2.0 * center[tile] - earlier + courant[x, tile, y] * total[tile]
                )
        return 0

    lax.fori_loop(0, rows_x, step, 0, unroll=4)
    wait_all(copies)
    add_sources(
        base, cells_here, samples_here, wavelet_here, 1, rows_x, rows_y, depth
    )


def sides(first, second, even, at_first, at_last):
    low = jnp.where(even, second, first)
    high = jnp.where(even, first, second)
    return jnp.where(at_first, 0.0, low), jnp.where(at_last, 0.0, high)


def add_halos(base, courant, x_first, x_second, y_first, y_second, x_halo, y_halo, rows, store):
    rows_x, tiles, rows_y, _ = base.shape
    y_tiles = rows_y // SUB
    even_x, first_x, last_x = parity("gx")
    even_y, first_y, last_y = parity("gy")
    zero = jnp.zeros((SUB, LANES), jnp.float32)
    for slot in range(HALO if x_halo is not None else 0):
        for tile in range(tiles):
            for y_tile in range(y_tiles):
                y = pl.ds(y_tile * SUB, SUB)
                low, high = sides(
                    x_first[slot, tile, y], x_second[slot, tile, y], even_x, first_x, last_x
                )
                x_halo[slot, tile, y] = low
                x_halo[HALO + slot, tile, y] = high

    def spread(x):
        for tile in range(tiles):
            where = (x, tile // 2, pl.ds(tile % 2 * HALO, HALO))
            low, high = sides(y_first[where], y_second[where], even_y, first_y, last_y)
            y_halo[x, tile, pl.ds(HALO, SUB)] = zero
            y_halo[x, tile, pl.ds(SUB, SUB)] = zero
            y_halo[x, tile, pl.ds(0, HALO)] = low
            y_halo[x, tile, pl.ds(2 * SUB, HALO)] = high

    def finish(x, x_terms):
        for y_tile in range(y_tiles):
            y = pl.ds(y_tile * SUB, SUB)
            done = []
            for tile in range(tiles):
                beyond = None
                terms = [(w, x_halo[slot, tile, y]) for w, slot in x_terms]
                for offset in range(1, HALO + 1):
                    weight = STENCIL_WEIGHTS[offset]
                    if y_tile == 0:
                        terms.append((weight, y_halo[x, tile, pl.ds(HALO - offset, SUB)]))
                    if y_tile == y_tiles - 1:
                        terms.append((weight, y_halo[x, tile, pl.ds(SUB + offset, SUB)]))
                for weight, value in terms:
                    beyond = weight * value if beyond is None else beyond + weight * value
                value = base[x, tile, y]
                if beyond is not None:
                    value = value + courant[x, tile, y] * beyond
                done.append(value)
            store(x, y_tile, done)

    for x in rows:
        spread(x)
    for x in rows:
        x_terms = []
        for offset in range(1, HALO + 1):
            if x - offset < 0:
                x_terms.append((STENCIL_WEIGHTS[offset], HALO + x - offset))
            if x + offset >= rows_x:
                x_terms.append((STENCIL_WEIGHTS[offset], HALO + x + offset - rows_x))
        finish(x, x_terms)


def inner_rows(rows_x):
    return range(HALO, rows_x - HALO)


def outer_rows(rows_x):
    return [*range(HALO), *range(rows_x - HALO, rows_x)]


def mid_kernel(
    base, courant, x_in, x_in_2, y_in, y_in_2, blank,
    padded, x_first, x_second, y_first, y_second, x_halo, y_halo,
):
    rows_x, tiles, rows_y, _ = base.shape
    even_x, _, _ = parity("gx")
    even_y, _, _ = parity("gy")

    def store(x, y_tile, values):
        for tile, value in enumerate(values):
            padded[x + HALO, tile, pl.ds(SUB + y_tile * SUB, SUB)] = value

    add_halos(
        base, courant, x_in, x_in_2, y_in, y_in_2, x_halo, y_halo, range(rows_x), store
    )
    field = padded_vector(padded)
    pack_x(field, range(HALO), range(rows_x - HALO, rows_x), even_x, x_first, x_second)

    def rows(x, tile):
        y = SUB + rows_y - HALO
        return padded[x + HALO, tile, pl.ds(SUB, HALO)], padded[x + HALO, tile, pl.ds(y, HALO)]

    pack_y(rows, rows_x, tiles, even_y, y_first, y_second)


def lift_depth(first, second):
    lane = iota(1)
    early = lax.rem(lane, 2) == 0
    tiles = range(len(first))
    even = [jnp.where(early, a, rolled(b, 1, 1)) for a, b in zip(first, second)]
    odd = [jnp.where(early, rolled(a, -1, 1), b) for a, b in zip(first, second)]
    for weight_odd, weight_even in ((LIFT_ALPHA, LIFT_BETA), (LIFT_GAMMA, LIFT_DELTA)):
        up = [rolled(value, -2, 1) for value in even]
        up.append(even[-1])
        above = [jnp.where(lane < LANES - 2, up[t], up[t + 1]) for t in tiles]
        odd = [odd[t] + weight_odd * (even[t] + above[t]) for t in tiles]
        down = [odd[0]] + [rolled(value, 2, 1) for value in odd]
        below = [jnp.where(lane >= 2, down[t + 1], down[t]) for t in tiles]
        even = [even[t] + weight_even * (odd[t] + below[t]) for t in tiles]
    return (
        [jnp.where(early, e, rolled(o, 1, 1)) for e, o in zip(even, odd)],
        [jnp.where(early, rolled(e, -1, 1), o) for e, o in zip(even, odd)],
    )


def next_kernel(
    base, courant, x_in, x_in_2, y_in, y_in_2,
    field, x_first, x_second, x_halo, y_halo,
):
    rows_x, tiles, rows_y, _ = base.shape
    even_x, _, _ = parity("gx")

    def store(x, y_tile, values):
        y = pl.ds(y_tile * SUB, SUB)
        for tile, value in enumerate(values):
            field[x, tile, y] = value

    add_halos(
        base, courant, x_in, x_in_2, y_in, y_in_2, x_halo, y_halo, outer_rows(rows_x), store
    )
    for y_tile in range(rows_y // SUB):
        y = pl.ds(y_tile * SUB, SUB)
        rows = []
        for tile in range(tiles):
            start = [field[x, tile, y] for x in range(3)]
            end = [field[x, tile, y] for x in range(rows_x - 4, rows_x)]
            low = (start[0], start[1] + LIFT_ALPHA * (start[0] + start[2]))
            high = (
                end[2] + LIFT_BETA * (end[1] + LIFT_ALPHA * (end[0] + end[2])),
                end[3] + LIFT_ALPHA * end[2],
            )
            rows.append(low + high)
        for slot in range(2):
            low, high = lift_depth(
                [row[slot] for row in rows], [row[2 + slot] for row in rows]
            )
            for tile in range(tiles):
                x_first[slot, tile, y] = jnp.where(even_x, high[tile], low[tile])
                x_second[slot, tile, y] = jnp.where(even_x, low[tile], high[tile])


def outward(field, out, sems):
    tiles = field.shape[1]
    return paired(
        [field.at[:, tile] for tile in range(tiles)],
        [out.at[:, :, pl.ds(tile * LANES, LANES)] for tile in range(tiles)],
        sems,
    )


def depth_kernel(base, courant, y_in, y_in_2, edges, field, lifted, out, y_halo, sems):
    rows_x, tiles, rows_y, _ = base.shape

    def store(x, y_tile, values):
        for tile, value in enumerate(values):
            field[x, tile, pl.ds(y_tile * SUB, SUB)] = value

    add_halos(
        base, courant, None, None, y_in, y_in_2, None, y_halo, inner_rows(rows_x), store
    )
    copies = start_all(outward(field, out, sems))

    def step(x, _):
        for y in range(0, rows_y, 2 * SUB):
            here = pl.ds(y, SUB), pl.ds(y + SUB, SUB)
            pair = lift_depth(
                *([field[x, tile, part] for tile in range(tiles)] for part in here)
            )
            for part, values in zip(here, pair):
                for tile, value in enumerate(values):
                    lifted[x, tile, part] = value
        return 0

    lax.fori_loop(0, rows_x, step, 0, unroll=4)
    wait_all(copies)


def lift_x_kernel(lifted, x_in, x_in_2, out, y_first, y_second):
    rows_x, tiles, rows_y, _ = lifted.shape
    y_tiles = rows_y // SUB
    half = rows_x // 2
    even_x, first_x, last_x = parity("gx")
    even_y, _, _ = parity("gy")

    for tile in range(tiles):
        for y_tile in range(y_tiles):
            y = pl.ds(y_tile * SUB, SUB)
            got = [
                (
                    jnp.where(even_x, x_in_2[slot, tile, y], x_in[slot, tile, y]),
                    jnp.where(even_x, x_in[slot, tile, y], x_in_2[slot, tile, y]),
                )
                for slot in range(2)
            ]
            even = [lifted[2 * i, tile, y] for i in range(half)]
            odd = [lifted[2 * i + 1, tile, y] for i in range(half)]
            beyond = jnp.where(last_x, even[-1], got[0][1])
            even.append(beyond)
            odd = [odd[i] + LIFT_ALPHA * (even[i] + even[i + 1]) for i in range(half)]
            before = got[1][0] + LIFT_ALPHA * even[0]
            odd = [jnp.where(first_x, odd[0], before)] + odd
            last = even.pop() + LIFT_BETA * (odd[-1] + got[1][1])
            even = [even[i] + LIFT_BETA * (odd[i] + odd[i + 1]) for i in range(half)]
            even.append(jnp.where(last_x, even[-1], last))
            start = got[0][0] + LIFT_BETA * odd[0]
            start = odd[0] + LIFT_GAMMA * (start + even[0])
            odd = [odd[i + 1] + LIFT_GAMMA * (even[i] + even[i + 1]) for i in range(half)]
            padded = [jnp.where(first_x, odd[0], start)] + odd
            even = [even[i] + LIFT_DELTA * (padded[i] + padded[i + 1]) for i in range(half)]
            here = pl.ds(SUB + y_tile * SUB, SUB)
            for i in range(half):
                out[2 * i, tile, here] = even[i]
                out[2 * i + 1, tile, here] = odd[i]

    head = lax.broadcasted_iota(jnp.int32, (2, LANES), 0) == 0

    def pack(x, _):
        for tile in range(tiles):

            def rows(y):
                return out[x, tile, pl.ds(SUB + y, 2)]

            low = rows(0)
            low = low + jnp.where(head, 0.0, LIFT_ALPHA * (rows(-1) + rows(1)))
            end = rows_y - 2
            high, below = rows(end), rows(end - 1)
            more = LIFT_BETA * (below + LIFT_ALPHA * (rows(end - 2) + high))
            high = high + jnp.where(head, more, LIFT_ALPHA * below)
            where = (x, tile // 4, pl.ds(tile % 4 * 2, 2))
            y_first[where] = jnp.where(even_y, high, low)
            y_second[where] = jnp.where(even_y, low, high)
        return 0

    lax.fori_loop(0, rows_x, pack, 0, unroll=8)


def y_scales():
    z_odd = lax.rem(iota(1), 2) == 1

    def scale(x_odd, y_odd):
        power = (1 if x_odd else -1) + (1 if y_odd else -1)
        return jnp.where(
            z_odd, LIFT_SCALE ** (power + 1) / QUANT_STEP, LIFT_SCALE ** (power - 1) / QUANT_STEP
        )

    return [[scale(x_odd, y_odd) for y_odd in (False, True)] for x_odd in (False, True)]


def lift_y_local_kernel(lifted, even_out, odd_out):
    rows_x, tiles, _, _ = lifted.shape
    _, first_y, last_y = parity("gy")
    sub = iota(0)
    top = sub == SUB - 1
    bottom = sub == 0
    at_first = bottom & first_y
    at_last = top & last_y
    scales = y_scales()

    def row(x, x_odd):
        for tile in range(tiles):
            even = lifted[x, tile, pl.ds(SUB, SUB, stride=2)]
            odd = lifted[x, tile, pl.ds(SUB + 1, SUB, stride=2)]
            beyond = jnp.where(at_last, even, jnp.where(top, 0.0, rolled(even, -1, 0)))
            odd = odd + LIFT_ALPHA * (even + beyond)
            before = LIFT_ALPHA * even
            under = jnp.where(at_first, odd, jnp.where(bottom, before, rolled(odd, 1, 0)))
            last = LIFT_BETA * odd
            even = even + LIFT_BETA * (odd + under)
            beyond = jnp.where(at_last, even, jnp.where(top, last, rolled(even, -1, 0)))
            start = before + LIFT_GAMMA * (LIFT_BETA * before + even)
            odd = odd + LIFT_GAMMA * (even + beyond)
            under = jnp.where(at_first, odd, jnp.where(bottom, start, rolled(odd, 1, 0)))
            even = even + LIFT_DELTA * (odd + under)
            even_out[x, tile] = even * scales[x_odd][0]
            odd_out[x, tile] = odd * scales[x_odd][1]

    def step(pair, _):
        row(2 * pair, 0)
        row(2 * pair + 1, 1)
        return 0

    lax.fori_loop(0, rows_x // 2, step, 0, unroll=2)


def lift_y_kernel(even_in, odd_in, y_in, y_in_2, out, codes, sems):
    rows_x, tiles, _, _ = even_in.shape
    even_y, first_y, last_y = parity("gy")
    sub = iota(0)
    edge = DEAD_ZONE / QUANT_STEP
    a, b, g, d = LIFT_ALPHA, LIFT_BETA, LIFT_GAMMA, LIFT_DELTA

    def at(places, keep):
        total = jnp.zeros((SUB, LANES), jnp.float32)
        for place, weight in places.items():
            total = jnp.where(sub == place, weight, total)
        return jnp.where(keep, total, 0.0)

    last = SUB - 1
    low = (
        (at({0: d * g}, ~first_y), at({}, ~first_y)),
        (
            at({0: b + d * (1.0 + 3.0 * g * b), 1: d * g * b}, ~first_y),
            at({0: g * b}, ~first_y),
        ),
    )
    far_odd = a + g * (1.0 + 2.0 * b * a)
    high = (
        (
            at({last: b * a + d * (g * b * a + far_odd), last - 1: d * g * b * a}, ~last_y),
            at({last: far_odd, last - 1: g * b * a}, ~last_y),
        ),
        (at({last: d * g * b}, ~last_y), at({last: g * b}, ~last_y)),
    )
    scales = y_scales()
    weights = [
        [
            [
                tuple(
                    jnp.where(even_y, one[slot][part], other[slot][part]) * scales[x_odd][part]
                    for part in range(2)
                )
                for slot in range(2)
            ]
            for one, other in ((high, low), (low, high))
        ]
        for x_odd in range(2)
    ]

    def code(value):
        return value - jnp.minimum(jnp.maximum(value, -edge), edge)

    def row(x, x_odd):
        for tile in range(tiles):
            even, odd = even_in[x, tile], odd_in[x, tile]
            for message, own in zip((y_in, y_in_2), weights[x_odd]):
                for slot in range(2):
                    place = pl.ds(tile % 4 * 2 + slot, 1)
                    value = jnp.broadcast_to(message[x, tile // 4, place], (SUB, LANES))
                    even = even + own[slot][0] * value
                    odd = odd + own[slot][1] * value
            codes[x, tile, pl.ds(0, SUB, stride=2)] = code(even)
            codes[x, tile, pl.ds(1, SUB, stride=2)] = code(odd)

    chunk = rows_x // 4
    copies = [
        [
            pltpu.make_async_copy(
                codes.at[pl.ds(part * chunk, chunk), tile],
                out.at[pl.ds(part * chunk, chunk), :, pl.ds(tile * LANES, LANES)],
                sems.at[part, tile],
            )
            for tile in range(tiles)
        ]
        for part in range(4)
    ]
    for part in range(4):
        for x in range(part * chunk, (part + 1) * chunk):
            row(x, x % 2)
        start_all(copies[part])
    for part in copies:
        wait_all(part)


def whole(count):
    return [pl.BlockSpec(memory_space=pltpu.VMEM)] * count


def far(count):
    return [pl.BlockSpec(memory_space=pltpu.HBM)] * count


def call(kernel, in_specs, out_specs, out_shape, scratch=(), cost=1.0, aliases=None, **kwargs):
    return pl.pallas_call(
        kernel,
        in_specs=in_specs,
        out_specs=out_specs,
        out_shape=[jax.ShapeDtypeStruct(shape, jnp.float32) for shape in out_shape],
        scratch_shapes=list(scratch),
        input_output_aliases=aliases or {},
        compiler_params=pltpu.CompilerParams(vmem_limit_bytes=16 << 20),
        cost_estimate=pl.CostEstimate(
            flops=int(cost * 1e6), bytes_accessed=int(cost * 1e6), transcendentals=0
        ),
        **kwargs,
    )


def swaps(names, counts, partner):
    pairs = []
    for y in range(counts[0]):
        for x in range(counts[1]):
            target = partner(y, x)
            pairs.append((y * counts[1] + x, target[0] * counts[1] + target[1]))
    return functools.partial(lax.ppermute, axis_name=names, perm=pairs)


def exchanges(count_y, count_x):
    names = ("gy", "gx")
    counts = (count_y, count_x)

    def second(index, count):
        return (index + 1) % count if index % 2 else (index - 1) % count

    x_first = swaps(names, counts, lambda y, x: (y, x ^ 1))
    x_second = swaps(names, counts, lambda y, x: (y, second(x, count_x)))
    y_first = swaps(names, counts, lambda y, x: (y ^ 1, x))

    def inner_y(y, x):
        return (second(y, count_y), x) if 0 < y < count_y - 1 else (y, x ^ 1)

    return x_first, x_second, y_first, swaps(names, counts, inner_y)


def shards(pressure_now, pressure_old, classes, class_table, wavelet, source_cells, samples):
    rows_x, rows_y, depth = pressure_now.shape
    tiles = depth // LANES
    swap_x, swap_x_2, swap_y, swap_y_2 = exchanges(lax.axis_size("gy"), lax.axis_size("gx"))
    padded_shape = (rows_x + 2 * HALO, tiles, rows_y + 2 * SUB, LANES)
    block_shape = (rows_x, tiles, rows_y, LANES)
    x_shape = (HALO, tiles, rows_y, LANES)
    y_shape = (rows_x, tiles // 2, SUB, LANES)
    x_lift_shape = (2, tiles, rows_y, LANES)
    y_lift_shape = (rows_x, tiles // 4, SUB, LANES)
    tall_shape = (rows_x, tiles, rows_y + 2 * SUB, LANES)
    half_shape = (rows_x, tiles, rows_y // 2, LANES)
    natural = (rows_x, rows_y, depth)
    sems = pltpu.SemaphoreType.DMA((tiles,))
    halos = (
        pltpu.VMEM((2 * HALO, tiles, rows_y, LANES), jnp.float32),
        pltpu.VMEM((rows_x, tiles, 3 * SUB, LANES), jnp.float32),
    )

    def star(sends):
        got = []
        for place, swap in enumerate((swap_x, swap_x_2, swap_y, swap_y_2)):
            got.append(swap(sends[place]))
        return got

    f32 = jnp.float32
    scalar_memory = (
        pltpu.SMEM(wavelet.shape, f32),
        pltpu.SMEM(source_cells.shape, jnp.int32),
        pltpu.SMEM(samples.shape, jnp.int32),
    )
    pressure_old, classes, class_table, wavelet, source_cells, samples = (
        pltpu.with_memory_space_constraint(array, pltpu.HBM)
        for array in (pressure_old, classes, class_table, wavelet, source_cells, samples)
    )
    sends = call(
        sends_kernel, whole(1), whole(4), [x_shape, x_shape, y_shape, y_shape], name="sends"
    )(pressure_now)
    got = star(sends)
    now, base, courant, blank = call(
        first_local_kernel, whole(1) + far(6), whole(4),
        [padded_shape, block_shape, block_shape, padded_shape],
        (
            pltpu.VMEM(natural, f32), pltpu.VMEM(natural, jnp.int32),
            pltpu.SMEM(class_table.shape, f32), *scalar_memory,
            pltpu.SemaphoreType.DMA((6,)),
        ),
        cost=4.0, name="first_local",
    )(pressure_now, pressure_old, classes, class_table, wavelet, source_cells, samples)
    mid, *sends = call(
        mid_kernel, whole(7), whole(5), [padded_shape, x_shape, x_shape, y_shape, y_shape],
        halos, aliases={6: 0}, name="mid",
    )(base, courant, *got, blank)
    got = star(sends)
    base, pressure_mid = call(
        second_local_kernel, whole(3) + far(3), whole(1) + far(1), [block_shape, natural],
        (*scalar_memory, pltpu.SemaphoreType.DMA((tiles + 3,))), cost=4.0, name="second_local",
    )(mid, now, courant, wavelet, source_cells, samples)
    field, *sends = call(
        next_kernel, whole(6), whole(3), [block_shape, x_lift_shape, x_lift_shape],
        halos, name="next",
    )(base, courant, *got)
    got_y = got[2:]
    got_2, got = swap_x_2(sends[1]), swap_x(sends[0])
    _, lifted, pressure_next = call(
        depth_kernel, whole(5), whole(2) + far(1), [block_shape, block_shape, natural],
        (halos[1], sems), cost=4.0, aliases={4: 0}, name="depth",
    )(base, courant, *got_y, field)
    lifted, *sends = call(
        lift_x_kernel, whole(3), whole(3), [tall_shape, y_lift_shape, y_lift_shape],
        name="lift_x",
    )(lifted, got, got_2)
    got, got_2 = swap_y(sends[0]), swap_y_2(sends[1])
    halves = call(
        lift_y_local_kernel, whole(1), whole(2), [half_shape, half_shape], cost=4.0,
        name="lift_y_local",
    )(lifted)
    (snapshot_code,) = call(
        lift_y_kernel, whole(4), far(1), [natural],
        (pltpu.VMEM(block_shape, f32), pltpu.SemaphoreType.DMA((4, tiles))), name="lift_y",
    )(*halves, got, got_2)
    return (pressure_next, pressure_mid, snapshot_code)


def solution(mesh):
    block = P(("shot", "gx"), "gy", None)
    return jax.shard_map(
        shards,
        mesh=mesh,
        in_specs=(block, block, block, P(), P("shot"), P("shot"), P("shot")),
        out_specs=(block, block, block),
        check_vma=False,
    )
```

profile of v0, /device:TPU:0, one launch (start us, length us, event | category | flops | bytes accessed | tf_op | source)
XLA Modules:
  0.0 30.1 jit_solution(17739689481933364199)
XLA Ops:
  0.6 1.0 %copy-done = f32[16,16,512]{2,1,0:T(8,128)S(1)} copy-done((f32[16,16,512]{2,1,0:T(8,128)S(1)}, f32[16,16,512]{2,1,0:T(8,128)}, u32[]{:S(2)}) %copy-start) | copy-done | bytes 524312
  1.7 0.1 sends.1
  1.8 0.6 %collective-permute-start = (f32[4,4,16,128]{3,2,1,0:T(8,128)S(1)}, f32[4,4,16,128]{3,2,1,0:T(8,128)S(1)}, u32[]{:S(2)}, u32[]{:S(2)}) collective-permute-start(f32[4,4,16,128]{3,2,1,0:T(8,128)S(1)} %get-tuple-element.30), channel_id=1, source_target_pairs={{0,1},{1,0},{2,3},{3,2},{4,5},{5,4},{6,7},{7,6},{8,9},{9,8},{10,11... | collective-permute-start | bytes 393224 | tf_op jit(solution)/shard_map/ppermute | solution.py:702
  2.3 2.6 %collective-permute-start.1 = (f32[4,4,16,128]{3,2,1,0:T(8,128)S(1)}, f32[4,4,16,128]{3,2,1,0:T(8,128)S(1)}, u32[]{:S(2)}, u32[]{:S(2)}) collective-permute-start(f32[4,4,16,128]{3,2,1,0:T(8,128)S(1)} %get-tuple-element.31), channel_id=1, source_target_pairs={{0,3},{1,2},{2,1},{3,0},{4,7},{5,6},{6,5},{7,4},{8,11},{9,10},{10,... | collective-permute-start | bytes 393224 | tf_op jit(solution)/shard_map/ppermute | solution.py:702
  4.9 1.6 %collective-permute-start.2 = (f32[16,2,8,128]{3,2,1,0:T(8,128)S(1)}, f32[16,2,8,128]{3,2,1,0:T(8,128)S(1)}, u32[]{:S(2)}, u32[]{:S(2)}) collective-permute-start(f32[16,2,8,128]{3,2,1,0:T(8,128)S(1)} %get-tuple-element.32), channel_id=1, source_target_pairs={{0,4},{1,5},{2,6},{3,7},{4,0},{5,1},{6,2},{7,3},{8,12},{9,13},{10,... | collective-permute-start | bytes 393224 | tf_op jit(solution)/shard_map/ppermute | solution.py:702
  6.5 2.4 %first_local.1 = (f32[24,4,32,128]{3,2,1,0:T(8,128)S(1)}, f32[16,4,16,128]{3,2,1,0:T(8,128)S(1)}, f32[16,4,16,128]{3,2,1,0:T(8,128)S(1)}, f32[24,4,32,128]{3,2,1,0:T(8,128)S(1)}) custom-call(f32[16,16,512]{2,1,0:T(8,128)S(1)} %copy-done, f32[16,16,512]{2,1,0:T(8,128)} %old.1, s32[16,16,512]{2,1,0:T(8,128)} %classes.1, f32[16]{0:T(128)} %table.1, ...), custom_call_target="tpu_custom_call" | custom-call | flops 4000000 | bytes 4000000 | tf_op jit(solution)/shard_map/first_local/pallas_call | solution.py:719
  9.0 1.4 %collective-permute-done.2.y_in = f32[16,2,8,128]{3,2,1,0:T(8,128)S(1)} collective-permute-done((f32[16,2,8,128]{3,2,1,0:T(8,128)S(1)}, f32[16,2,8,128]{3,2,1,0:T(8,128)S(1)}, u32[]{:S(2)}, u32[]{:S(2)}) %collective-permute-start.2) | collective-permute-done | bytes 131104 | tf_op jit(solution)/shard_map/ppermute | solution.py:702
  10.4 0.4 %mid.1 = (f32[24,4,32,128]{3,2,1,0:T(8,128)S(1)}, f32[4,4,16,128]{3,2,1,0:T(8,128)S(1)}, f32[4,4,16,128]{3,2,1,0:T(8,128)S(1)}, f32[16,2,8,128]{3,2,1,0:T(8,128)S(1)}, f32[16,2,8,128]{3,2,1,0:T(8,128)S(1)}) custom-call(f32[16,4,16,128]{3,2,1,0:T(8,128)S(1)} %get-tuple-element.28.base, ...), custom_call_target="tpu_custom_call", output_to_operand_aliasing={{0}: (6, {})} | custom-call | flops 1000000 | bytes 1000000 | tf_op jit(solution)/shard_map/mid/pallas_call | solution.py:729
  10.8 2.8 %collective-permute-start.4 = (f32[16,2,8,128]{3,2,1,0:T(8,128)S(1)}, f32[16,2,8,128]{3,2,1,0:T(8,128)S(1)}, u32[]{:S(2)}, u32[]{:S(2)}) collective-permute-start(f32[16,2,8,128]{3,2,1,0:T(8,128)S(1)} %get-tuple-element.38), channel_id=1, source_target_pairs={{0,4},{1,5},{2,6},{3,7},{4,0},{5,1},{6,2},{7,3},{8,12},{9,13},{10,... | collective-permute-start | bytes 393224 | tf_op jit(solution)/shard_map/ppermute | solution.py:702
  13.6 0.5 %collective-permute-start.6 = (f32[4,4,16,128]{3,2,1,0:T(8,128)S(1)}, f32[4,4,16,128]{3,2,1,0:T(8,128)S(1)}, u32[]{:S(2)}, u32[]{:S(2)}) collective-permute-start(f32[4,4,16,128]{3,2,1,0:T(8,128)S(1)} %get-tuple-element.40), channel_id=1, source_target_pairs={{0,1},{1,0},{2,3},{3,2},{4,5},{5,4},{6,7},{7,6},{8,9},{9,8},{10,11... | collective-permute-start | bytes 393224 | tf_op jit(solution)/shard_map/ppermute | solution.py:702
  14.1 0.1 collective-permute-start.7
  14.2 1.7 %second_local.1 = (f32[16,4,16,128]{3,2,1,0:T(8,128)S(1)}, f32[16,16,512]{2,1,0:T(8,128)}) custom-call(f32[24,4,32,128]{3,2,1,0:T(8,128)S(1)} %get-tuple-element.35.padded, f32[24,4,32,128]{3,2,1,0:T(8,128)S(1)} %get-tuple-element.36.before, f32[16,4,16,128]{3,2,1,0:T(8,128)S(1)} %get-tuple-element.29.courant, f32[256]{0:T(256)} %wavelet.3, s32[4]{0:T(128)} %cells.3, ...), custom_call_target="tpu_custom_call" | custom-call | flops 4000000 | bytes 4000000 | tf_op jit(solution)/shard_map/second_local/pallas_call | solution.py:734
  15.9 0.6 %collective-permute-done.4.y_in = f32[16,2,8,128]{3,2,1,0:T(8,128)S(1)} collective-permute-done((f32[16,2,8,128]{3,2,1,0:T(8,128)S(1)}, f32[16,2,8,128]{3,2,1,0:T(8,128)S(1)}, u32[]{:S(2)}, u32[]{:S(2)}) %collective-permute-start.4) | collective-permute-done | bytes 131104 | tf_op jit(solution)/shard_map/ppermute | solution.py:702
  16.5 3.2 %collective-permute-done.7.x_in_2 = f32[4,4,16,128]{3,2,1,0:T(8,128)S(1)} collective-permute-done((f32[4,4,16,128]{3,2,1,0:T(8,128)S(1)}, f32[4,4,16,128]{3,2,1,0:T(8,128)S(1)}, u32[]{:S(2)}, u32[]{:S(2)}) %collective-permute-start.7) | collective-permute-done | bytes 131104 | tf_op jit(solution)/shard_map/ppermute | solution.py:702
  19.7 0.6 %next.1 = (f32[16,4,16,128]{3,2,1,0:T(8,128)S(1)}, f32[2,4,16,128]{3,2,1,0:T(8,128)S(1)}, f32[2,4,16,128]{3,2,1,0:T(8,128)S(1)}) custom-call(f32[16,4,16,128]{3,2,1,0:T(8,128)S(1)} %get-tuple-element.37.base, f32[16,4,16,128]{3,2,1,0:T(8,128)S(1)} %get-tuple-element.29.courant, f32[4,4,16,128]{3,2,1,0:T(8,128)S(1)} %collective-permute-done.6.x_in, ...), custom_call_target="tpu_custom_call" | custom-call | flops 1000000 | bytes 1000000 | tf_op jit(solution)/shard_map/next/pallas_call | solution.py:738
  20.3 0.2 collective-permute-start.8
  20.5 0.5 %collective-permute-start.9 = (f32[2,4,16,128]{3,2,1,0:T(8,128)S(1)}, f32[2,4,16,128]{3,2,1,0:T(8,128)S(1)}, u32[]{:S(2)}, u32[]{:S(2)}) collective-permute-start(f32[2,4,16,128]{3,2,1,0:T(8,128)S(1)} %get-tuple-element.47), channel_id=1, source_target_pairs={{0,3},{1,2},{2,1},{3,0},{4,7},{5,6},{6,5},{7,4},{8,11},{9,10},{10,... | collective-permute-start | bytes 196616 | tf_op jit(solution)/shard_map/ppermute | solution.py:743
  21.0 1.9 %depth.1 = (f32[16,4,16,128]{3,2,1,0:T(8,128)S(1)}, f32[16,4,16,128]{3,2,1,0:T(8,128)S(1)}, f32[16,16,512]{2,1,0:T(8,128)}) custom-call(f32[16,4,16,128]{3,2,1,0:T(8,128)S(1)} %get-tuple-element.37.base, f32[16,4,16,128]{3,2,1,0:T(8,128)S(1)} %get-tuple-element.29.courant, ...), custom_call_target="tpu_custom_call", output_to_operand_aliasing={{0}: (4, {})} | custom-call | flops 4000000 | bytes 4000000 | tf_op jit(solution)/shard_map/depth/pallas_call | solution.py:744
  23.0 1.3 %collective-permute-done.9.x_in_2 = f32[2,4,16,128]{3,2,1,0:T(8,128)S(1)} collective-permute-done((f32[2,4,16,128]{3,2,1,0:T(8,128)S(1)}, f32[2,4,16,128]{3,2,1,0:T(8,128)S(1)}, u32[]{:S(2)}, u32[]{:S(2)}) %collective-permute-start.9) | collective-permute-done | bytes 65568 | tf_op jit(solution)/shard_map/ppermute | solution.py:743
  24.3 0.3 lift_x.1
  24.6 1.8 %collective-permute-start.10 = (f32[16,1,8,128]{3,2,1,0:T(8,128)S(1)}, f32[16,1,8,128]{3,2,1,0:T(8,128)S(1)}, u32[]{:S(2)}, u32[]{:S(2)}) collective-permute-start(f32[16,1,8,128]{3,2,1,0:T(8,128)S(1)} %get-tuple-element.51), channel_id=1, source_target_pairs={{0,4},{1,5},{2,6},{3,7},{4,0},{5,1},{6,2},{7,3},{8,12},{9,13},{10,... | collective-permute-start | bytes 196616 | tf_op jit(solution)/shard_map/ppermute | solution.py:752
  26.4 0.3 %lift_y_local.1 = (f32[16,4,8,128]{3,2,1,0:T(8,128)S(1)}, f32[16,4,8,128]{3,2,1,0:T(8,128)S(1)}) custom-call(f32[16,4,32,128]{3,2,1,0:T(8,128)S(1)} %get-tuple-element.48.lifted), custom_call_target="tpu_custom_call" | custom-call | flops 4000000 | bytes 4000000 | tf_op jit(solution)/shard_map/lift_y_local/pallas_call | solution.py:753
  26.7 2.3 %collective-permute-done.10.y_in = f32[16,1,8,128]{3,2,1,0:T(8,128)S(1)} collective-permute-done((f32[16,1,8,128]{3,2,1,0:T(8,128)S(1)}, f32[16,1,8,128]{3,2,1,0:T(8,128)S(1)}, u32[]{:S(2)}, u32[]{:S(2)}) %collective-permute-start.10) | collective-permute-done | bytes 65568 | tf_op jit(solution)/shard_map/ppermute | solution.py:752
  29.1 1.0 %lift_y.1 = f32[16,16,512]{2,1,0:T(8,128)} custom-call(f32[16,4,8,128]{3,2,1,0:T(8,128)S(1)} %get-tuple-element.49.even_in, f32[16,4,8,128]{3,2,1,0:T(8,128)S(1)} %get-tuple-element.50.odd_in, f32[16,1,8,128]{3,2,1,0:T(8,128)S(1)} %collective-permute-done.10.y_in, f32[16,1,8,128]{3,2,1,0:T(8,128)S(1)} %collective-permute-done.11.y_in_2), custom_call_target="tpu_custom_call" | custom-call | flops 1000000 | bytes 1000000 | tf_op jit(solution)/shard_map/lift_y/pallas_call | solution.py:757
  (11 shorter events, 0.0 us)
Async XLA Ops:
  0.6 1.0 %copy-start = (f32[16,16,512]{2,1,0:T(8,128)S(1)}, f32[16,16,512]{2,1,0:T(8,128)}, u32[]{:S(2)}) copy-start(f32[16,16,512]{2,1,0:T(8,128)} %now.3) | copy-start | bytes 1572868
  1.8 7.2 %collective-permute-start = (f32[4,4,16,128]{3,2,1,0:T(8,128)S(1)}, f32[4,4,16,128]{3,2,1,0:T(8,128)S(1)}, u32[]{:S(2)}, u32[]{:S(2)}) collective-permute-start(f32[4,4,16,128]{3,2,1,0:T(8,128)S(1)} %get-tuple-element.30), channel_id=1, source_target_pairs={{0,1},{1,0},{2,3},{3,2},{4,5},{5,4},{6,7},{7,6},{8,9},{9,8},{10,11... | collective-permute-start | bytes 393224 | tf_op jit(solution)/shard_map/ppermute | solution.py:702
  2.3 6.6 %collective-permute-start.1 = (f32[4,4,16,128]{3,2,1,0:T(8,128)S(1)}, f32[4,4,16,128]{3,2,1,0:T(8,128)S(1)}, u32[]{:S(2)}, u32[]{:S(2)}) collective-permute-start(f32[4,4,16,128]{3,2,1,0:T(8,128)S(1)} %get-tuple-element.31), channel_id=1, source_target_pairs={{0,3},{1,2},{2,1},{3,0},{4,7},{5,6},{6,5},{7,4},{8,11},{9,10},{10,... | collective-permute-start | bytes 393224 | tf_op jit(solution)/shard_map/ppermute | solution.py:702
  4.9 5.5 %collective-permute-start.2 = (f32[16,2,8,128]{3,2,1,0:T(8,128)S(1)}, f32[16,2,8,128]{3,2,1,0:T(8,128)S(1)}, u32[]{:S(2)}, u32[]{:S(2)}) collective-permute-start(f32[16,2,8,128]{3,2,1,0:T(8,128)S(1)} %get-tuple-element.32), channel_id=1, source_target_pairs={{0,4},{1,5},{2,6},{3,7},{4,0},{5,1},{6,2},{7,3},{8,12},{9,13},{10,... | collective-permute-start | bytes 393224 | tf_op jit(solution)/shard_map/ppermute | solution.py:702
  6.5 3.9 %collective-permute-start.3 = (f32[16,2,8,128]{3,2,1,0:T(8,128)S(1)}, f32[16,2,8,128]{3,2,1,0:T(8,128)S(1)}, u32[]{:S(2)}, u32[]{:S(2)}) collective-permute-start(f32[16,2,8,128]{3,2,1,0:T(8,128)S(1)} %get-tuple-element.33), channel_id=1, source_target_pairs={{0,1},{1,0},{2,3},{3,2},{4,8},{5,9},{6,10},{7,11},{8,4},{9,5},{10,... | collective-permute-start | bytes 393224 | tf_op jit(solution)/shard_map/ppermute | solution.py:702
  10.8 5.7 %collective-permute-start.4 = (f32[16,2,8,128]{3,2,1,0:T(8,128)S(1)}, f32[16,2,8,128]{3,2,1,0:T(8,128)S(1)}, u32[]{:S(2)}, u32[]{:S(2)}) collective-permute-start(f32[16,2,8,128]{3,2,1,0:T(8,128)S(1)} %get-tuple-element.38), channel_id=1, source_target_pairs={{0,4},{1,5},{2,6},{3,7},{4,0},{5,1},{6,2},{7,3},{8,12},{9,13},{10,... | collective-permute-start | bytes 393224 | tf_op jit(solution)/shard_map/ppermute | solution.py:702
  13.6 3.0 %collective-permute-start.5 = (f32[16,2,8,128]{3,2,1,0:T(8,128)S(1)}, f32[16,2,8,128]{3,2,1,0:T(8,128)S(1)}, u32[]{:S(2)}, u32[]{:S(2)}) collective-permute-start(f32[16,2,8,128]{3,2,1,0:T(8,128)S(1)} %get-tuple-element.39), channel_id=1, source_target_pairs={{0,1},{1,0},{2,3},{3,2},{4,8},{5,9},{6,10},{7,11},{8,4},{9,5},{10,... | collective-permute-start | bytes 393224 | tf_op jit(solution)/shard_map/ppermute | solution.py:702
  13.6 3.0 %collective-permute-start.6 = (f32[4,4,16,128]{3,2,1,0:T(8,128)S(1)}, f32[4,4,16,128]{3,2,1,0:T(8,128)S(1)}, u32[]{:S(2)}, u32[]{:S(2)}) collective-permute-start(f32[4,4,16,128]{3,2,1,0:T(8,128)S(1)} %get-tuple-element.40), channel_id=1, source_target_pairs={{0,1},{1,0},{2,3},{3,2},{4,5},{5,4},{6,7},{7,6},{8,9},{9,8},{10,11... | collective-permute-start | bytes 393224 | tf_op jit(solution)/shard_map/ppermute | solution.py:702
  14.1 5.6 %collective-permute-start.7 = (f32[4,4,16,128]{3,2,1,0:T(8,128)S(1)}, f32[4,4,16,128]{3,2,1,0:T(8,128)S(1)}, u32[]{:S(2)}, u32[]{:S(2)}) collective-permute-start(f32[4,4,16,128]{3,2,1,0:T(8,128)S(1)} %get-tuple-element.41), channel_id=1, source_target_pairs={{0,3},{1,2},{2,1},{3,0},{4,7},{5,6},{6,5},{7,4},{8,11},{9,10},{10,... | collective-permute-start | bytes 393224 | tf_op jit(solution)/shard_map/ppermute | solution.py:702
  20.3 2.7 %collective-permute-start.8 = (f32[2,4,16,128]{3,2,1,0:T(8,128)S(1)}, f32[2,4,16,128]{3,2,1,0:T(8,128)S(1)}, u32[]{:S(2)}, u32[]{:S(2)}) collective-permute-start(f32[2,4,16,128]{3,2,1,0:T(8,128)S(1)} %get-tuple-element.46), channel_id=1, source_target_pairs={{0,1},{1,0},{2,3},{3,2},{4,5},{5,4},{6,7},{7,6},{8,9},{9,8},{10,11... | collective-permute-start | bytes 196616 | tf_op jit(solution)/shard_map/ppermute | solution.py:743
  20.5 3.8 %collective-permute-start.9 = (f32[2,4,16,128]{3,2,1,0:T(8,128)S(1)}, f32[2,4,16,128]{3,2,1,0:T(8,128)S(1)}, u32[]{:S(2)}, u32[]{:S(2)}) collective-permute-start(f32[2,4,16,128]{3,2,1,0:T(8,128)S(1)} %get-tuple-element.47), channel_id=1, source_target_pairs={{0,3},{1,2},{2,1},{3,0},{4,7},{5,6},{6,5},{7,4},{8,11},{9,10},{10,... | collective-permute-start | bytes 196616 | tf_op jit(solution)/shard_map/ppermute | solution.py:743
  24.6 4.5 %collective-permute-start.10 = (f32[16,1,8,128]{3,2,1,0:T(8,128)S(1)}, f32[16,1,8,128]{3,2,1,0:T(8,128)S(1)}, u32[]{:S(2)}, u32[]{:S(2)}) collective-permute-start(f32[16,1,8,128]{3,2,1,0:T(8,128)S(1)} %get-tuple-element.51), channel_id=1, source_target_pairs={{0,4},{1,5},{2,6},{3,7},{4,0},{5,1},{6,2},{7,3},{8,12},{9,13},{10,... | collective-permute-start | bytes 196616 | tf_op jit(solution)/shard_map/ppermute | solution.py:752
  26.4 2.7 %collective-permute-start.11 = (f32[16,1,8,128]{3,2,1,0:T(8,128)S(1)}, f32[16,1,8,128]{3,2,1,0:T(8,128)S(1)}, u32[]{:S(2)}, u32[]{:S(2)}) collective-permute-start(f32[16,1,8,128]{3,2,1,0:T(8,128)S(1)} %get-tuple-element.52), channel_id=1, source_target_pairs={{0,1},{1,0},{2,3},{3,2},{4,8},{5,9},{6,10},{7,11},{8,4},{9,5},{10,... | collective-permute-start | bytes 196616 | tf_op jit(solution)/shard_map/ppermute | solution.py:752
where the time goes:
time: 30.3 us; the launch traced here: 30.1 us
  starting transfers between devices  10.7 us (35%)
  waiting for transfers between devices  8.91 us (29%)
  Pallas kernels  8.79 us (29%)
  local copies, waits for them, and re-layouts  1.03 us (3%)
  between operations  0.73 us (2%)
    ppermute x8, starting transfers between devices, star(): got.append(swap(sends[place]))  8.15 us
    ppermute x8, waiting for transfers between devices, star(): got.append(swap(sends[place]))  5.25 us
    pallas_call x1, Pallas kernels, shards(): call(first_local_kernel, whole(1) + far(6), whole(4), [padded_shape, bloc...  2.43 us
    ppermute x2, waiting for transfers between devices, shards(): got, got_2 = (swap_y(sends[0]), swap_y_2(sends[1]))  2.35 us
    pallas_call x1, Pallas kernels, shards(): call(depth_kernel, whole(5), whole(2) + far(1), [block_shape, block_shape...  1.95 us
    ppermute x2, starting transfers between devices, shards(): got, got_2 = (swap_y(sends[0]), swap_y_2(sends[1]))  1.79 us
    pallas_call x1, Pallas kernels, shards(): call(second_local_kernel, whole(3) + far(3), whole(1) + far(1), [block_sh...  1.66 us
    ppermute x2, waiting for transfers between devices, shards(): got_2, got = (swap_x_2(sends[1]), swap_x(sends[0]))  1.32 us
  transfers between devices with their start and end apart: 12, of which 5 were waited for; matrix products, arithmetic and copies ran while one was open for 0% of the time, Pallas kernels for 21%

commit v1 on v0

--- a/solution.py
+++ b/solution.py
@@ -252,10 +252,9 @@
     )
 
 
-def sides(first, second, even, at_first, at_last):
-    low = jnp.where(even, second, first)
-    high = jnp.where(even, first, second)
-    return jnp.where(at_first, 0.0, low), jnp.where(at_last, 0.0, high)
+def sides(first, second, even, at_end):
+    second = jnp.where(at_end, 0.0, second)
+    return jnp.where(even, second, first), jnp.where(even, first, second)
 
 
 def add_halos(base, courant, x_first, x_second, y_first, y_second, x_halo, y_halo, rows, store):
@@ -263,21 +262,21 @@
     y_tiles = rows_y // SUB
     even_x, first_x, last_x = parity("gx")
     even_y, first_y, last_y = parity("gy")
+    end_x, end_y = first_x | last_x, first_y | last_y
+    first_at = jnp.where(even_x, HALO, 0)
     zero = jnp.zeros((SUB, LANES), jnp.float32)
     for slot in range(HALO if x_halo is not None else 0):
         for tile in range(tiles):
             for y_tile in range(y_tiles):
                 y = pl.ds(y_tile * SUB, SUB)
-                low, high = sides(
-                    x_first[slot, tile, y], x_second[slot, tile, y], even_x, first_x, last_x
-                )
-                x_halo[slot, tile, y] = low
-                x_halo[HALO + slot, tile, y] = high
+                x_halo[first_at + slot, tile, y] = x_first[slot, tile, y]
+                second = x_second[slot, tile, y]
+                x_halo[HALO - first_at + slot, tile, y] = jnp.where(end_x, 0.0, second)
 
     def spread(x):
         for tile in range(tiles):
             where = (x, tile // 2, pl.ds(tile % 2 * HALO, HALO))
-            low, high = sides(y_first[where], y_second[where], even_y, first_y, last_y)
+            low, high = sides(y_first[where], y_second[where], even_y, end_y)
             y_halo[x, tile, pl.ds(HALO, SUB)] = zero
             y_halo[x, tile, pl.ds(SUB, SUB)] = zero
             y_halo[x, tile, pl.ds(0, HALO)] = low
@@ -512,7 +511,7 @@
     return [[scale(x_odd, y_odd) for y_odd in (False, True)] for x_odd in (False, True)]
 
 
-def lift_y_local_kernel(lifted, even_out, odd_out):
+def lift_y_local_kernel(lifted, out):
     rows_x, tiles, _, _ = lifted.shape
     _, first_y, last_y = parity("gy")
     sub = iota(0)
@@ -537,8 +536,8 @@
             odd = odd + LIFT_GAMMA * (even + beyond)
             under = jnp.where(at_first, odd, jnp.where(bottom, start, rolled(odd, 1, 0)))
             even = even + LIFT_DELTA * (odd + under)
-            even_out[x, tile] = even * scales[x_odd][0]
-            odd_out[x, tile] = odd * scales[x_odd][1]
+            out[x, tile, pl.ds(0, SUB, stride=2)] = even * scales[x_odd][0]
+            out[x, tile, pl.ds(1, SUB, stride=2)] = odd * scales[x_odd][1]
 
     def step(pair, _):
         row(2 * pair, 0)
@@ -548,83 +547,62 @@
     lax.fori_loop(0, rows_x // 2, step, 0, unroll=2)
 
 
-def lift_y_kernel(even_in, odd_in, y_in, y_in_2, out, codes, sems):
-    rows_x, tiles, _, _ = even_in.shape
+def lift_y_kernel(local, y_in, y_in_2, out, codes, low_rows, high_rows, sems):
+    rows_x, tiles, rows_y, _ = local.shape
     even_y, first_y, last_y = parity("gy")
     sub = iota(0)
     edge = DEAD_ZONE / QUANT_STEP
     a, b, g, d = LIFT_ALPHA, LIFT_BETA, LIFT_GAMMA, LIFT_DELTA
-
-    def at(places, keep):
+    far_odd = a + g * (1.0 + 2.0 * b * a)
+    added = (
+        ({0: d * g}, {0: b + d * (1.0 + 3.0 * g * b), 1: g * b, 2: d * g * b}),
+        (
+            {4: d * g * b * a, 5: g * b * a, 6: b * a + d * (g * b * a + far_odd), 7: far_odd},
+            {6: d * g * b, 7: g * b},
+        ),
+    )
+
+    def at(places, keep, scale):
         total = jnp.zeros((SUB, LANES), jnp.float32)
         for place, weight in places.items():
             total = jnp.where(sub == place, weight, total)
-        return jnp.where(keep, total, 0.0)
-
-    last = SUB - 1
-    low = (
-        (at({0: d * g}, ~first_y), at({}, ~first_y)),
-        (
-            at({0: b + d * (1.0 + 3.0 * g * b), 1: d * g * b}, ~first_y),
-            at({0: g * b}, ~first_y),
-        ),
-    )
-    far_odd = a + g * (1.0 + 2.0 * b * a)
-    high = (
-        (
-            at({last: b * a + d * (g * b * a + far_odd), last - 1: d * g * b * a}, ~last_y),
-            at({last: far_odd, last - 1: g * b * a}, ~last_y),
-        ),
-        (at({last: d * g * b}, ~last_y), at({last: g * b}, ~last_y)),
-    )
-    scales = y_scales()
+        return jnp.where(keep, total * scale, 0.0)
+
     weights = [
         [
-            [
-                tuple(
-                    jnp.where(even_y, one[slot][part], other[slot][part]) * scales[x_odd][part]
-                    for part in range(2)
-                )
-                for slot in range(2)
-            ]
-            for one, other in ((high, low), (low, high))
+            [at(places, keep, jnp.where(lax.rem(sub, 2) == 1, odd, even)) for places in rows]
+            for rows, keep in zip(added, (~first_y, ~last_y))
         ]
-        for x_odd in range(2)
+        for even, odd in y_scales()
     ]
 
-    def code(value):
-        return value - jnp.minimum(jnp.maximum(value, -edge), edge)
-
-    def row(x, x_odd):
-        for tile in range(tiles):
-            even, odd = even_in[x, tile], odd_in[x, tile]
-            for message, own in zip((y_in, y_in_2), weights[x_odd]):
+    def row(x):
+        for group in range(y_in.shape[1]):
+            first, second = y_in[x, group], y_in_2[x, group]
+            low_rows[x, group] = jnp.where(even_y, second, first)
+            high_rows[x, group] = jnp.where(even_y, first, second)
+        for tile in range(tiles):
+            for side, (rows, y) in enumerate(((low_rows, 0), (high_rows, rows_y - SUB))):
+                value = local[x, tile, pl.ds(y, SUB)]
                 for slot in range(2):
                     place = pl.ds(tile % 4 * 2 + slot, 1)
-                    value = jnp.broadcast_to(message[x, tile // 4, place], (SUB, LANES))
-                    even = even + own[slot][0] * value
-                    odd = odd + own[slot][1] * value
-            codes[x, tile, pl.ds(0, SUB, stride=2)] = code(even)
-            codes[x, tile, pl.ds(1, SUB, stride=2)] = code(odd)
+                    beyond = jnp.broadcast_to(rows[x, tile // 4, place], (SUB, LANES))
+                    value = value + weights[x % 2][side][slot] * beyond
+                codes[x, pl.ds(y, SUB), pl.ds(tile * LANES, LANES)] = value - jnp.minimum(
+                    jnp.maximum(value, -edge), edge
+                )
 
     chunk = rows_x // 4
-    copies = [
-        [
-            pltpu.make_async_copy(
-                codes.at[pl.ds(part * chunk, chunk), tile],
-                out.at[pl.ds(part * chunk, chunk), :, pl.ds(tile * LANES, LANES)],
-                sems.at[part, tile],
-            )
-            for tile in range(tiles)
-        ]
-        for part in range(4)
-    ]
+    copies = paired(
+        [codes.at[pl.ds(part * chunk, chunk)] for part in range(4)],
+        [out.at[pl.ds(part * chunk, chunk)] for part in range(4)],
+        sems,
+    )
     for part in range(4):
         for x in range(part * chunk, (part + 1) * chunk):
-            row(x, x % 2)
-        start_all(copies[part])
-    for part in copies:
-        wait_all(part)
+            row(x)
+        copies[part].start()
+    wait_all(copies)
 
 
 def whole(count):
@@ -680,6 +658,7 @@
 def shards(pressure_now, pressure_old, classes, class_table, wavelet, source_cells, samples):
     rows_x, rows_y, depth = pressure_now.shape
     tiles = depth // LANES
+    assert rows_y == 2 * SUB and tiles % 4 == 0
     swap_x, swap_x_2, swap_y, swap_y_2 = exchanges(lax.axis_size("gy"), lax.axis_size("gx"))
     padded_shape = (rows_x + 2 * HALO, tiles, rows_y + 2 * SUB, LANES)
     block_shape = (rows_x, tiles, rows_y, LANES)
@@ -688,7 +667,6 @@
     x_lift_shape = (2, tiles, rows_y, LANES)
     y_lift_shape = (rows_x, tiles // 4, SUB, LANES)
     tall_shape = (rows_x, tiles, rows_y + 2 * SUB, LANES)
-    half_shape = (rows_x, tiles, rows_y // 2, LANES)
     natural = (rows_x, rows_y, depth)
     sems = pltpu.SemaphoreType.DMA((tiles,))
     halos = (
@@ -750,14 +728,17 @@
         name="lift_x",
     )(lifted, got, got_2)
     got, got_2 = swap_y(sends[0]), swap_y_2(sends[1])
-    halves = call(
-        lift_y_local_kernel, whole(1), whole(2), [half_shape, half_shape], cost=4.0,
-        name="lift_y_local",
+    (local,) = call(
+        lift_y_local_kernel, whole(1), whole(1), [block_shape], cost=4.0, name="lift_y_local"
     )(lifted)
     (snapshot_code,) = call(
-        lift_y_kernel, whole(4), far(1), [natural],
-        (pltpu.VMEM(block_shape, f32), pltpu.SemaphoreType.DMA((4, tiles))), name="lift_y",
-    )(*halves, got, got_2)
+        lift_y_kernel, whole(3), far(1), [natural],
+        (
+            pltpu.VMEM(natural, f32), pltpu.VMEM(y_lift_shape, f32), pltpu.VMEM(y_lift_shape, f32),
+            pltpu.SemaphoreType.DMA((4,)),
+        ),
+        name="lift_y",
+    )(local, got, got_2)
     return (pressure_next, pressure_mid, snapshot_code)
 
 

time: 30.3 us -> 30.1 us (level)
  no operation moved by 1% of the time
where the time goes in v1:
time: 30.1 us; the launch traced here: 29.9 us
  starting transfers between devices  10.7 us (36%)
  waiting for transfers between devices  8.92 us (30%)
  Pallas kernels  8.61 us (29%)
  local copies, waits for them, and re-layouts  1.03 us (3%)
  between operations  0.73 us (2%)
    ppermute x8, starting transfers between devices, star(): got.append(swap(sends[place]))  8.15 us
    ppermute x8, waiting for transfers between devices, star(): got.append(swap(sends[place]))  5.25 us
    pallas_call x1, Pallas kernels, shards(): call(first_local_kernel, whole(1) + far(6), whole(4), [padded_shape, bloc...  2.43 us
    ppermute x2, waiting for transfers between devices, shards(): got, got_2 = (swap_y(sends[0]), swap_y_2(sends[1]))  2.35 us
    pallas_call x1, Pallas kernels, shards(): call(depth_kernel, whole(5), whole(2) + far(1), [block_shape, block_shape...  1.94 us
    ppermute x2, starting transfers between devices, shards(): got, got_2 = (swap_y(sends[0]), swap_y_2(sends[1]))  1.79 us
    pallas_call x1, Pallas kernels, shards(): call(second_local_kernel, whole(3) + far(3), whole(1) + far(1), [block_sh...  1.66 us
    ppermute x2, waiting for transfers between devices, shards(): got_2, got = (swap_x_2(sends[1]), swap_x(sends[0]))  1.32 us
  transfers between devices with their start and end apart: 12, of which 5 were waited for; matrix products, arithmetic and copies ran while one was open for 0% of the time, Pallas kernels for 21%

profile of v1, /device:TPU:0, one launch (start us, length us, event | category | flops | bytes accessed | tf_op | source)
XLA Modules:
  0.0 29.9 jit_solution(1835841016839241848)
XLA Ops:
  0.6 1.0 %copy-done = f32[16,16,512]{2,1,0:T(8,128)S(1)} copy-done((f32[16,16,512]{2,1,0:T(8,128)S(1)}, f32[16,16,512]{2,1,0:T(8,128)}, u32[]{:S(2)}) %copy-start) | copy-done | bytes 524312
  1.7 0.1 sends.1
  1.8 0.6 %collective-permute-start = (f32[4,4,16,128]{3,2,1,0:T(8,128)S(1)}, f32[4,4,16,128]{3,2,1,0:T(8,128)S(1)}, u32[]{:S(2)}, u32[]{:S(2)}) collective-permute-start(f32[4,4,16,128]{3,2,1,0:T(8,128)S(1)} %get-tuple-element.28), channel_id=1, source_target_pairs={{0,1},{1,0},{2,3},{3,2},{4,5},{5,4},{6,7},{7,6},{8,9},{9,8},{10,11... | collective-permute-start | bytes 393224 | tf_op jit(solution)/shard_map/ppermute | solution.py:680
  2.3 2.6 %collective-permute-start.1 = (f32[4,4,16,128]{3,2,1,0:T(8,128)S(1)}, f32[4,4,16,128]{3,2,1,0:T(8,128)S(1)}, u32[]{:S(2)}, u32[]{:S(2)}) collective-permute-start(f32[4,4,16,128]{3,2,1,0:T(8,128)S(1)} %get-tuple-element.29), channel_id=1, source_target_pairs={{0,3},{1,2},{2,1},{3,0},{4,7},{5,6},{6,5},{7,4},{8,11},{9,10},{10,... | collective-permute-start | bytes 393224 | tf_op jit(solution)/shard_map/ppermute | solution.py:680
  4.9 1.6 %collective-permute-start.2 = (f32[16,2,8,128]{3,2,1,0:T(8,128)S(1)}, f32[16,2,8,128]{3,2,1,0:T(8,128)S(1)}, u32[]{:S(2)}, u32[]{:S(2)}) collective-permute-start(f32[16,2,8,128]{3,2,1,0:T(8,128)S(1)} %get-tuple-element.30), channel_id=1, source_target_pairs={{0,4},{1,5},{2,6},{3,7},{4,0},{5,1},{6,2},{7,3},{8,12},{9,13},{10,... | collective-permute-start | bytes 393224 | tf_op jit(solution)/shard_map/ppermute | solution.py:680
  6.5 2.4 %first_local.1 = (f32[24,4,32,128]{3,2,1,0:T(8,128)S(1)}, f32[16,4,16,128]{3,2,1,0:T(8,128)S(1)}, f32[16,4,16,128]{3,2,1,0:T(8,128)S(1)}, f32[24,4,32,128]{3,2,1,0:T(8,128)S(1)}) custom-call(f32[16,16,512]{2,1,0:T(8,128)S(1)} %copy-done, f32[16,16,512]{2,1,0:T(8,128)} %old.1, s32[16,16,512]{2,1,0:T(8,128)} %classes.1, f32[16]{0:T(128)} %table.1, ...), custom_call_target="tpu_custom_call" | custom-call | flops 4000000 | bytes 4000000 | tf_op jit(solution)/shard_map/first_local/pallas_call | solution.py:697
  9.0 1.4 %collective-permute-done.2.y_in = f32[16,2,8,128]{3,2,1,0:T(8,128)S(1)} collective-permute-done((f32[16,2,8,128]{3,2,1,0:T(8,128)S(1)}, f32[16,2,8,128]{3,2,1,0:T(8,128)S(1)}, u32[]{:S(2)}, u32[]{:S(2)}) %collective-permute-start.2) | collective-permute-done | bytes 131104 | tf_op jit(solution)/shard_map/ppermute | solution.py:680
  10.4 0.4 %mid.1 = (f32[24,4,32,128]{3,2,1,0:T(8,128)S(1)}, f32[4,4,16,128]{3,2,1,0:T(8,128)S(1)}, f32[4,4,16,128]{3,2,1,0:T(8,128)S(1)}, f32[16,2,8,128]{3,2,1,0:T(8,128)S(1)}, f32[16,2,8,128]{3,2,1,0:T(8,128)S(1)}) custom-call(f32[16,4,16,128]{3,2,1,0:T(8,128)S(1)} %get-tuple-element.26.base, ...), custom_call_target="tpu_custom_call", output_to_operand_aliasing={{0}: (6, {})} | custom-call | flops 1000000 | bytes 1000000 | tf_op jit(solution)/shard_map/mid/pallas_call | solution.py:707
  10.8 2.8 %collective-permute-start.4 = (f32[16,2,8,128]{3,2,1,0:T(8,128)S(1)}, f32[16,2,8,128]{3,2,1,0:T(8,128)S(1)}, u32[]{:S(2)}, u32[]{:S(2)}) collective-permute-start(f32[16,2,8,128]{3,2,1,0:T(8,128)S(1)} %get-tuple-element.36), channel_id=1, source_target_pairs={{0,4},{1,5},{2,6},{3,7},{4,0},{5,1},{6,2},{7,3},{8,12},{9,13},{10,... | collective-permute-start | bytes 393224 | tf_op jit(solution)/shard_map/ppermute | solution.py:680
  13.6 0.5 %collective-permute-start.6 = (f32[4,4,16,128]{3,2,1,0:T(8,128)S(1)}, f32[4,4,16,128]{3,2,1,0:T(8,128)S(1)}, u32[]{:S(2)}, u32[]{:S(2)}) collective-permute-start(f32[4,4,16,128]{3,2,1,0:T(8,128)S(1)} %get-tuple-element.38), channel_id=1, source_target_pairs={{0,1},{1,0},{2,3},{3,2},{4,5},{5,4},{6,7},{7,6},{8,9},{9,8},{10,11... | collective-permute-start | bytes 393224 | tf_op jit(solution)/shard_map/ppermute | solution.py:680
  14.1 0.1 collective-permute-start.7
  14.2 1.7 %second_local.1 = (f32[16,4,16,128]{3,2,1,0:T(8,128)S(1)}, f32[16,16,512]{2,1,0:T(8,128)}) custom-call(f32[24,4,32,128]{3,2,1,0:T(8,128)S(1)} %get-tuple-element.33.padded, f32[24,4,32,128]{3,2,1,0:T(8,128)S(1)} %get-tuple-element.34.before, f32[16,4,16,128]{3,2,1,0:T(8,128)S(1)} %get-tuple-element.27.courant, f32[256]{0:T(256)} %wavelet.3, s32[4]{0:T(128)} %cells.3, ...), custom_call_target="tpu_custom_call" | custom-call | flops 4000000 | bytes 4000000 | tf_op jit(solution)/shard_map/second_local/pallas_call | solution.py:712
  15.9 0.6 %collective-permute-done.4.y_in = f32[16,2,8,128]{3,2,1,0:T(8,128)S(1)} collective-permute-done((f32[16,2,8,128]{3,2,1,0:T(8,128)S(1)}, f32[16,2,8,128]{3,2,1,0:T(8,128)S(1)}, u32[]{:S(2)}, u32[]{:S(2)}) %collective-permute-start.4) | collective-permute-done | bytes 131104 | tf_op jit(solution)/shard_map/ppermute | solution.py:680
  16.5 3.2 %collective-permute-done.7.x_in_2 = f32[4,4,16,128]{3,2,1,0:T(8,128)S(1)} collective-permute-done((f32[4,4,16,128]{3,2,1,0:T(8,128)S(1)}, f32[4,4,16,128]{3,2,1,0:T(8,128)S(1)}, u32[]{:S(2)}, u32[]{:S(2)}) %collective-permute-start.7) | collective-permute-done | bytes 131104 | tf_op jit(solution)/shard_map/ppermute | solution.py:680
  19.7 0.6 %next.1 = (f32[16,4,16,128]{3,2,1,0:T(8,128)S(1)}, f32[2,4,16,128]{3,2,1,0:T(8,128)S(1)}, f32[2,4,16,128]{3,2,1,0:T(8,128)S(1)}) custom-call(f32[16,4,16,128]{3,2,1,0:T(8,128)S(1)} %get-tuple-element.35.base, f32[16,4,16,128]{3,2,1,0:T(8,128)S(1)} %get-tuple-element.27.courant, f32[4,4,16,128]{3,2,1,0:T(8,128)S(1)} %collective-permute-done.6.x_in, ...), custom_call_target="tpu_custom_call" | custom-call | flops 1000000 | bytes 1000000 | tf_op jit(solution)/shard_map/next/pallas_call | solution.py:716
  20.3 0.2 collective-permute-start.8
  20.5 0.5 %collective-permute-start.9 = (f32[2,4,16,128]{3,2,1,0:T(8,128)S(1)}, f32[2,4,16,128]{3,2,1,0:T(8,128)S(1)}, u32[]{:S(2)}, u32[]{:S(2)}) collective-permute-start(f32[2,4,16,128]{3,2,1,0:T(8,128)S(1)} %get-tuple-element.45), channel_id=1, source_target_pairs={{0,3},{1,2},{2,1},{3,0},{4,7},{5,6},{6,5},{7,4},{8,11},{9,10},{10,... | collective-permute-start | bytes 196616 | tf_op jit(solution)/shard_map/ppermute | solution.py:721
  21.0 1.9 %depth.1 = (f32[16,4,16,128]{3,2,1,0:T(8,128)S(1)}, f32[16,4,16,128]{3,2,1,0:T(8,128)S(1)}, f32[16,16,512]{2,1,0:T(8,128)}) custom-call(f32[16,4,16,128]{3,2,1,0:T(8,128)S(1)} %get-tuple-element.35.base, f32[16,4,16,128]{3,2,1,0:T(8,128)S(1)} %get-tuple-element.27.courant, ...), custom_call_target="tpu_custom_call", output_to_operand_aliasing={{0}: (4, {})} | custom-call | flops 4000000 | bytes 4000000 | tf_op jit(solution)/shard_map/depth/pallas_call | solution.py:722
  23.0 1.3 %collective-permute-done.9.x_in_2 = f32[2,4,16,128]{3,2,1,0:T(8,128)S(1)} collective-permute-done((f32[2,4,16,128]{3,2,1,0:T(8,128)S(1)}, f32[2,4,16,128]{3,2,1,0:T(8,128)S(1)}, u32[]{:S(2)}, u32[]{:S(2)}) %collective-permute-start.9) | collective-permute-done | bytes 65568 | tf_op jit(solution)/shard_map/ppermute | solution.py:721
  24.3 0.3 lift_x.1
  24.6 1.8 %collective-permute-start.10 = (f32[16,1,8,128]{3,2,1,0:T(8,128)S(1)}, f32[16,1,8,128]{3,2,1,0:T(8,128)S(1)}, u32[]{:S(2)}, u32[]{:S(2)}) collective-permute-start(f32[16,1,8,128]{3,2,1,0:T(8,128)S(1)} %get-tuple-element.47), channel_id=1, source_target_pairs={{0,4},{1,5},{2,6},{3,7},{4,0},{5,1},{6,2},{7,3},{8,12},{9,13},{10,... | collective-permute-start | bytes 196616 | tf_op jit(solution)/shard_map/ppermute | solution.py:730
  26.4 0.3 %lift_y_local.1.local = f32[16,4,16,128]{3,2,1,0:T(8,128)S(1)} custom-call(f32[16,4,32,128]{3,2,1,0:T(8,128)S(1)} %get-tuple-element.46.lifted), custom_call_target="tpu_custom_call" | custom-call | flops 4000000 | bytes 4000000 | tf_op jit(solution)/shard_map/lift_y_local/pallas_call | solution.py:731
  26.7 2.3 %collective-permute-done.10.y_in = f32[16,1,8,128]{3,2,1,0:T(8,128)S(1)} collective-permute-done((f32[16,1,8,128]{3,2,1,0:T(8,128)S(1)}, f32[16,1,8,128]{3,2,1,0:T(8,128)S(1)}, u32[]{:S(2)}, u32[]{:S(2)}) %collective-permute-start.10) | collective-permute-done | bytes 65568 | tf_op jit(solution)/shard_map/ppermute | solution.py:730
  29.1 0.9 %lift_y.1 = f32[16,16,512]{2,1,0:T(8,128)} custom-call(f32[16,4,16,128]{3,2,1,0:T(8,128)S(1)} %lift_y_local.1.local, f32[16,1,8,128]{3,2,1,0:T(8,128)S(1)} %collective-permute-done.10.y_in, f32[16,1,8,128]{3,2,1,0:T(8,128)S(1)} %collective-permute-done.11.y_in_2), custom_call_target="tpu_custom_call" | custom-call | flops 1000000 | bytes 1000000 | tf_op jit(solution)/shard_map/lift_y/pallas_call | solution.py:734
  (11 shorter events, 0.0 us)
Async XLA Ops:
  0.6 1.0 %copy-start = (f32[16,16,512]{2,1,0:T(8,128)S(1)}, f32[16,16,512]{2,1,0:T(8,128)}, u32[]{:S(2)}) copy-start(f32[16,16,512]{2,1,0:T(8,128)} %now.3) | copy-start | bytes 1572868
  1.8 7.2 %collective-permute-start = (f32[4,4,16,128]{3,2,1,0:T(8,128)S(1)}, f32[4,4,16,128]{3,2,1,0:T(8,128)S(1)}, u32[]{:S(2)}, u32[]{:S(2)}) collective-permute-start(f32[4,4,16,128]{3,2,1,0:T(8,128)S(1)} %get-tuple-element.28), channel_id=1, source_target_pairs={{0,1},{1,0},{2,3},{3,2},{4,5},{5,4},{6,7},{7,6},{8,9},{9,8},{10,11... | collective-permute-start | bytes 393224 | tf_op jit(solution)/shard_map/ppermute | solution.py:680
  2.3 6.6 %collective-permute-start.1 = (f32[4,4,16,128]{3,2,1,0:T(8,128)S(1)}, f32[4,4,16,128]{3,2,1,0:T(8,128)S(1)}, u32[]{:S(2)}, u32[]{:S(2)}) collective-permute-start(f32[4,4,16,128]{3,2,1,0:T(8,128)S(1)} %get-tuple-element.29), channel_id=1, source_target_pairs={{0,3},{1,2},{2,1},{3,0},{4,7},{5,6},{6,5},{7,4},{8,11},{9,10},{10,... | collective-permute-start | bytes 393224 | tf_op jit(solution)/shard_map/ppermute | solution.py:680
  4.9 5.5 %collective-permute-start.2 = (f32[16,2,8,128]{3,2,1,0:T(8,128)S(1)}, f32[16,2,8,128]{3,2,1,0:T(8,128)S(1)}, u32[]{:S(2)}, u32[]{:S(2)}) collective-permute-start(f32[16,2,8,128]{3,2,1,0:T(8,128)S(1)} %get-tuple-element.30), channel_id=1, source_target_pairs={{0,4},{1,5},{2,6},{3,7},{4,0},{5,1},{6,2},{7,3},{8,12},{9,13},{10,... | collective-permute-start | bytes 393224 | tf_op jit(solution)/shard_map/ppermute | solution.py:680
  6.5 3.9 %collective-permute-start.3 = (f32[16,2,8,128]{3,2,1,0:T(8,128)S(1)}, f32[16,2,8,128]{3,2,1,0:T(8,128)S(1)}, u32[]{:S(2)}, u32[]{:S(2)}) collective-permute-start(f32[16,2,8,128]{3,2,1,0:T(8,128)S(1)} %get-tuple-element.31), channel_id=1, source_target_pairs={{0,1},{1,0},{2,3},{3,2},{4,8},{5,9},{6,10},{7,11},{8,4},{9,5},{10,... | collective-permute-start | bytes 393224 | tf_op jit(solution)/shard_map/ppermute | solution.py:680
  10.8 5.7 %collective-permute-start.4 = (f32[16,2,8,128]{3,2,1,0:T(8,128)S(1)}, f32[16,2,8,128]{3,2,1,0:T(8,128)S(1)}, u32[]{:S(2)}, u32[]{:S(2)}) collective-permute-start(f32[16,2,8,128]{3,2,1,0:T(8,128)S(1)} %get-tuple-element.36), channel_id=1, source_target_pairs={{0,4},{1,5},{2,6},{3,7},{4,0},{5,1},{6,2},{7,3},{8,12},{9,13},{10,... | collective-permute-start | bytes 393224 | tf_op jit(solution)/shard_map/ppermute | solution.py:680
  13.6 3.0 %collective-permute-start.5 = (f32[16,2,8,128]{3,2,1,0:T(8,128)S(1)}, f32[16,2,8,128]{3,2,1,0:T(8,128)S(1)}, u32[]{:S(2)}, u32[]{:S(2)}) collective-permute-start(f32[16,2,8,128]{3,2,1,0:T(8,128)S(1)} %get-tuple-element.37), channel_id=1, source_target_pairs={{0,1},{1,0},{2,3},{3,2},{4,8},{5,9},{6,10},{7,11},{8,4},{9,5},{10,... | collective-permute-start | bytes 393224 | tf_op jit(solution)/shard_map/ppermute | solution.py:680
  13.6 3.0 %collective-permute-start.6 = (f32[4,4,16,128]{3,2,1,0:T(8,128)S(1)}, f32[4,4,16,128]{3,2,1,0:T(8,128)S(1)}, u32[]{:S(2)}, u32[]{:S(2)}) collective-permute-start(f32[4,4,16,128]{3,2,1,0:T(8,128)S(1)} %get-tuple-element.38), channel_id=1, source_target_pairs={{0,1},{1,0},{2,3},{3,2},{4,5},{5,4},{6,7},{7,6},{8,9},{9,8},{10,11... | collective-permute-start | bytes 393224 | tf_op jit(solution)/shard_map/ppermute | solution.py:680
  14.1 5.6 %collective-permute-start.7 = (f32[4,4,16,128]{3,2,1,0:T(8,128)S(1)}, f32[4,4,16,128]{3,2,1,0:T(8,128)S(1)}, u32[]{:S(2)}, u32[]{:S(2)}) collective-permute-start(f32[4,4,16,128]{3,2,1,0:T(8,128)S(1)} %get-tuple-element.39), channel_id=1, source_target_pairs={{0,3},{1,2},{2,1},{3,0},{4,7},{5,6},{6,5},{7,4},{8,11},{9,10},{10,... | collective-permute-start | bytes 393224 | tf_op jit(solution)/shard_map/ppermute | solution.py:680
  20.3 2.7 %collective-permute-start.8 = (f32[2,4,16,128]{3,2,1,0:T(8,128)S(1)}, f32[2,4,16,128]{3,2,1,0:T(8,128)S(1)}, u32[]{:S(2)}, u32[]{:S(2)}) collective-permute-start(f32[2,4,16,128]{3,2,1,0:T(8,128)S(1)} %get-tuple-element.44), channel_id=1, source_target_pairs={{0,1},{1,0},{2,3},{3,2},{4,5},{5,4},{6,7},{7,6},{8,9},{9,8},{10,11... | collective-permute-start | bytes 196616 | tf_op jit(solution)/shard_map/ppermute | solution.py:721
  20.5 3.8 %collective-permute-start.9 = (f32[2,4,16,128]{3,2,1,0:T(8,128)S(1)}, f32[2,4,16,128]{3,2,1,0:T(8,128)S(1)}, u32[]{:S(2)}, u32[]{:S(2)}) collective-permute-start(f32[2,4,16,128]{3,2,1,0:T(8,128)S(1)} %get-tuple-element.45), channel_id=1, source_target_pairs={{0,3},{1,2},{2,1},{3,0},{4,7},{5,6},{6,5},{7,4},{8,11},{9,10},{10,... | collective-permute-start | bytes 196616 | tf_op jit(solution)/shard_map/ppermute | solution.py:721
  24.6 4.5 %collective-permute-start.10 = (f32[16,1,8,128]{3,2,1,0:T(8,128)S(1)}, f32[16,1,8,128]{3,2,1,0:T(8,128)S(1)}, u32[]{:S(2)}, u32[]{:S(2)}) collective-permute-start(f32[16,1,8,128]{3,2,1,0:T(8,128)S(1)} %get-tuple-element.47), channel_id=1, source_target_pairs={{0,4},{1,5},{2,6},{3,7},{4,0},{5,1},{6,2},{7,3},{8,12},{9,13},{10,... | collective-permute-start | bytes 196616 | tf_op jit(solution)/shard_map/ppermute | solution.py:730
  26.4 2.7 %collective-permute-start.11 = (f32[16,1,8,128]{3,2,1,0:T(8,128)S(1)}, f32[16,1,8,128]{3,2,1,0:T(8,128)S(1)}, u32[]{:S(2)}, u32[]{:S(2)}) collective-permute-start(f32[16,1,8,128]{3,2,1,0:T(8,128)S(1)} %get-tuple-element.48), channel_id=1, source_target_pairs={{0,1},{1,0},{2,3},{3,2},{4,8},{5,9},{6,10},{7,11},{8,4},{9,5},{10,... | collective-permute-start | bytes 196616 | tf_op jit(solution)/shard_map/ppermute | solution.py:730
